TPU v7x, 512 devices: a whole 4x8x8 slice. The times are simulated.
512 devices in a mesh: lon: 8 (over y_lo, core), lat: 64 (over x, y_hi, z).
Axes of the slice: x: 4, y: 8 (y_hi: 2, y_lo: 4; y = y_hi * 4 + y_lo), z: 8, core: 2. Of those that a mesh axis runs over, the one named last changes fastest.
Arguments:
- ocean_state: bfloat16 [1, 384, 512, 256], P(None, 'lat', 'lon'), may hold values from -6 to 6
- land_sea: int32 [1, 384, 512], P(None, 'lat', 'lon'), may hold values 0 or 1
- cotangent: bfloat16 [1, 384, 512, 256], P(None, 'lat', 'lon'), may hold values from -6 to 6
- dw_kernel: float32 [7, 7, 256], replicated, may hold values from -0.875 to 0.875
- dw_bias: float32 [256], replicated, may hold values from -3 to 3
- ln_gain: float32 [256], replicated, may hold values from 0.1 to 1.9
- ln_bias: float32 [256], replicated, may hold values from -2 to 2
- w_in: bfloat16 [256, 1024], replicated, may hold values from -0.375 to 0.375
- b_in: float32 [1024], replicated, may hold values from -2 to 2
- w_out: bfloat16 [1024, 256], replicated, may hold values from -0.1875 to 0.1875
- b_out: float32 [256], replicated, may hold values from -2 to 2
- layer_scale: float32 [256], replicated, may hold values from 0.3 to 1.5
Outputs:
- output: bfloat16 [1, 384, 512, 256], P(None, 'lat', 'lon')
- grad_state: bfloat16 [1, 384, 512, 256], P(None, 'lat', 'lon')
- grad_kernel: float32 [7, 7, 256], replicated
- grad_dw_bias: float32 [256], replicated
- grad_ln_gain: float32 [256], replicated
- grad_ln_bias: float32 [256], replicated
- grad_w_in: float32 [256, 1024], replicated
- grad_b_in: float32 [1024], replicated
- grad_w_out: float32 [1024, 256], replicated
- grad_b_out: float32 [256], replicated
- grad_scale: float32 [256], replicated
All inputs are finite; a program needn't handle non-finite values. No bound on the sum of `land_sea` on one device may be relied on, other than what follows from the above.
Results may differ from a plain program's by a relative error of at most 0.0085.
Values may be sent and summed in bfloat16 or wider, within the bound.
No kernel may reach another device: no remote copies, remote signals or barrier semaphores. Data moves between devices by JAX's collectives and lax.ppermute only.
A program may use at most 64 MiB of HBM per device.

v0:
```python
import jax
import jax.numpy as jnp
from jax import lax
from jax.sharding import PartitionSpec as P


def extended(array, sides, width, wrap):
    for axis, dim in sides:
        size, length = (lax.axis_size(axis), array.shape[dim])
        up = [(i, (i + 1) % size) for i in range(size if wrap else size - 1)]
        down = [(j, i) for i, j in up]
        last = lax.slice_in_dim(array, length - width, length, axis=dim)
        leading = lax.slice_in_dim(array, 0, width, axis=dim)
        before = lax.ppermute(last, axis, up)
        after = lax.ppermute(leading, axis, down)
        array = jnp.concatenate([before, array, after], axis=dim)
    return array


def depthwise(padded, kernel, num_rows, num_cols):
    summed = jnp.zeros((padded.shape[0], num_rows, num_cols, padded.shape[3]), jnp.float32)
    for row_off in range(7):
        for col_off in range(7):
            summed = (
                summed
                + padded[:, row_off : row_off + num_rows, col_off : col_off + num_cols, :].astype(
                    jnp.float32
                )
                * kernel[row_off, col_off]
            )
    return summed


def transposed(padded, kernel, num_rows, num_cols):
    summed = jnp.zeros((padded.shape[0], num_rows, num_cols, padded.shape[3]), jnp.float32)
    for row_off in range(7):
        for col_off in range(7):
            summed = (
                summed
                + padded[
                    :, 6 - row_off : 6 - row_off + num_rows, 6 - col_off : 6 - col_off + num_cols, :
                ].astype(jnp.float32)
                * kernel[row_off, col_off]
            )
    return summed


def kernel_terms(padded, grad_depth, num_rows, num_cols):
    grad_float = grad_depth.astype(jnp.float32)
    rows_out = []
    for row_off in range(7):
        cols_out = []
        for col_off in range(7):
            window = padded[
                :, row_off : row_off + num_rows, col_off : col_off + num_cols, :
            ].astype(jnp.float32)
            cols_out.append(jnp.sum(window * grad_float, axis=(0, 1, 2)))
        rows_out.append(jnp.stack(cols_out))
    return jnp.stack(rows_out)


def forward_tokens(depth_out, ln_gain, ln_bias, w_in, b_in, w_out, b_out):
    center = depth_out - jnp.mean(depth_out, axis=-1, keepdims=True)
    inv_std = lax.rsqrt(jnp.mean(center * center, axis=-1, keepdims=True) + 1e-06)
    norm_hat = center * inv_std
    normed = (norm_hat * ln_gain + ln_bias).astype(jnp.bfloat16)
    pre_act = jnp.dot(normed, w_in, preferred_element_type=jnp.float32) + b_in
    activated = jax.nn.gelu(pre_act, approximate=True).astype(jnp.bfloat16)
    branch = jnp.dot(activated, w_out, preferred_element_type=jnp.float32) + b_out
    return (norm_hat, inv_std, normed, pre_act, activated, branch)


def backward_tokens(masked, norm_hat, inv_std, pre_act, ln_gain, w_in, w_out, layer_scale):
    grad_branch = (masked * layer_scale).astype(jnp.bfloat16)
    grad_act = lax.dot_general(
        grad_branch, w_out, (((1,), (1,)), ((), ())), preferred_element_type=jnp.float32
    )
    unused, pull_back = jax.vjp(lambda v: jax.nn.gelu(v, approximate=True), pre_act)
    grad_pre = pull_back(grad_act)[0].astype(jnp.bfloat16)
    grad_norm = lax.dot_general(
        grad_pre, w_in, (((1,), (1,)), ((), ())), preferred_element_type=jnp.float32
    )
    scaled = grad_norm * ln_gain
    grad_depth = (
        inv_std
        * (
            scaled
            - jnp.mean(scaled, axis=-1, keepdims=True)
            - norm_hat * jnp.mean(scaled * norm_hat, axis=-1, keepdims=True)
        )
    ).astype(jnp.bfloat16)
    return (grad_branch, grad_pre, grad_norm, grad_depth)


def weight_terms(masked, branch, grad_branch, activated, normed, grad_pre, grad_norm, norm_hat):
    dims = (((0,), (0,)), ((), ()))
    grad_w_in = lax.dot_general(normed, grad_pre, dims, preferred_element_type=jnp.float32)
    grad_w_out = lax.dot_general(activated, grad_branch, dims, preferred_element_type=jnp.float32)
    return (
        grad_w_in,
        grad_w_out,
        jnp.sum(grad_pre.astype(jnp.float32), axis=0),
        jnp.sum(grad_branch.astype(jnp.float32), axis=0),
        jnp.sum(masked * branch, axis=0),
        jnp.sum(grad_norm * norm_hat, axis=0),
        jnp.sum(grad_norm, axis=0),
    )


def local(
    ocean_state,
    land_sea,
    cotangent,
    dw_kernel,
    dw_bias,
    ln_gain,
    ln_bias,
    w_in,
    b_in,
    w_out,
    b_out,
    layer_scale,
):
    num_batch, num_rows, num_cols, channels = ocean_state.shape
    mask_float = land_sea.astype(jnp.float32)[..., None]
    lon_ext = extended(ocean_state, (("lon", 2),), 3, True)
    padded = extended(lon_ext, (("lat", 1),), 3, False)
    depth_out = depthwise(padded, dw_kernel, num_rows, num_cols) + dw_bias
    masked = (mask_float * cotangent.astype(jnp.float32)).reshape(-1, channels)
    norm_hat, inv_std, normed, pre_act, activated, branch = forward_tokens(
        depth_out.reshape(-1, channels), ln_gain, ln_bias, w_in, b_in, w_out, b_out
    )
    grad_branch, grad_pre, grad_norm, grad_flat = backward_tokens(
        masked, norm_hat, inv_std, pre_act, ln_gain, w_in, w_out, layer_scale
    )
    grad_terms = weight_terms(
        masked, branch, grad_branch, activated, normed, grad_pre, grad_norm, norm_hat
    )
    grad_depth = grad_flat.reshape(num_batch, num_rows, num_cols, channels)
    grad_ext = extended(grad_depth, (("lon", 2),), 3, True)
    grad_pad = extended(grad_ext, (("lat", 1),), 3, False)
    branch_own = branch.reshape(num_batch, num_rows, num_cols, channels)
    output = (ocean_state.astype(jnp.float32) + mask_float * layer_scale * branch_own).astype(
        jnp.bfloat16
    )
    grad_state = (
        cotangent.astype(jnp.float32) + transposed(grad_pad, dw_kernel, num_rows, num_cols)
    ).astype(jnp.bfloat16)
    kernel_part = kernel_terms(padded, grad_depth, num_rows, num_cols)
    bias_part = jnp.sum(grad_depth.astype(jnp.float32), axis=(0, 1, 2))
    grad_w_in, grad_w_out, grad_b_in, grad_b_out, grad_scale, grad_ln_gain, grad_ln_bias = (
        grad_terms
    )
    reduced = lax.psum(
        (
            grad_w_in,
            grad_w_out,
            grad_b_in,
            grad_b_out,
            grad_scale,
            grad_ln_gain,
            grad_ln_bias,
            kernel_part,
            bias_part,
        ),
        ("lon", "lat"),
    )
    (
        grad_w_in,
        grad_w_out,
        grad_b_in,
        grad_b_out,
        grad_scale,
        grad_ln_gain,
        grad_ln_bias,
        kernel_part,
        bias_part,
    ) = reduced
    all_cells = num_batch * num_rows * num_cols * lax.axis_size("lon") * lax.axis_size("lat")
    factor = 1.0 / jnp.sqrt(jnp.float32(all_cells))
    return (
        output,
        grad_state,
        kernel_part * factor,
        bias_part * factor,
        grad_ln_gain * factor,
        grad_ln_bias * factor,
        grad_w_in * factor,
        grad_b_in * factor,
        grad_w_out * factor,
        grad_b_out * factor,
        grad_scale * factor,
    )


def solution(mesh):
    in_specs = (
        P(None, "lat", "lon", None),
        P(None, "lat", "lon"),
        P(None, "lat", "lon", None),
        P(),
        P(),
        P(),
        P(),
        P(),
        P(),
        P(),
        P(),
        P(),
    )
    out_specs = (
        P(None, "lat", "lon", None),
        P(None, "lat", "lon", None),
        P(),
        P(),
        P(),
        P(),
        P(),
        P(),
        P(),
        P(),
        P(),
    )
    return jax.shard_map(local, mesh=mesh, in_specs=in_specs, out_specs=out_specs, check_vma=False)
```

profile of v0, /device:TPU:1, one launch (start us, length us, event | category | flops | bytes accessed | tf_op | source)
XLA Modules:
  0.0 450.9 jit_solution(3544239886626899903)
XLA Ops:
  8.1 8.8 %collective-permute-start.1 = (bf16[1,6,3,256]{3,2,1,0:T(4,128)(2,1)S(1)}, bf16[1,6,3,256]{3,2,1,0:T(4,128)(2,1)S(1)}, u32[]{:S(2)}, u32[]{:S(2)}) collective-permute-start(bf16[1,6,3,256]{3,2,1,0:T(4,128)(2,1)S(1)} %get-tuple-element.102), channel_id=1, source_target_pairs={{64,0},{128,64},{192,128},{256,192},{320,256},{384,320},{448,384},... | collective-permute-start | bytes 27656 | tf_op jit(solution)/shard_map/ppermute | solution.py:15
  16.9 1.9 collective-permute-start
  18.8 0.9 fusion.150
  19.8 1.0 fusion.148
  20.8 1.0 fusion.149
  21.8 0.9 constant_dynamic-update-slice_fusion.1
  23.4 1.0 pad_maximum_fusion.2
  24.5 1.3 collective-permute-start.2
  25.8 1.3 collective-permute-start.3
  27.5 3.8 collective-permute-done.3
  31.4 3.2 fusion.142
  37.6 1.3 convert_reduce_fusion
  41.2 1.4 fusion.151
  42.7 1.7 fusion.141
  44.4 3.6 collective-permute-start.4
  48.0 2.6 collective-permute-start.5
  51.6 111.9 %all-reduce = (f32[7,7,256]{2,1,0:T(8,128)S(1)}, f32[256]{0:T(256)S(1)}, f32[256]{0:T(256)S(1)}, f32[256]{0:T(256)S(1)}, f32[1024]{0:T(1024)S(1)}, /*index=5*/f32[256]{0:T(256)S(1)}, f32[256]{0:T(256)S(1)}) all-reduce(f32[7,7,256]{2,1,0:T(8,128)S(1)} %constant_dynamic-update-slice_fusion.2, ...), channel_id=1, replica_groups=mesh['lon'=8,'lat'=64] {'lon','lat'}, use_global_device_ids=true, to_apply=%region_53.0 | all-reduce | flops 14848 | bytes 118784 | tf_op jit(solution)/shard_map/psum | solution.py:154
  167.1 1.3 collective-permute-start.6
  168.4 4.0 collective-permute-start.7
  173.0 1.2 collective-permute-done.7
  174.3 3.8 fusion.55
  178.0 262.5 %all-reduce.4.cloned.1.call-done = (f32[256,1024]{1,0:T(8,128)}, f32[1024,256]{1,0:T(8,128)}) async-done(((f32[256,1024]{1,0:T(8,128)}, f32[1024,256]{1,0:T(8,128)}), (f32[256,1024]{1,0:T(8,128)}, f32[1024,256]{1,0:T(8,128)})) %all-reduce.4.cloned.1.call-update) | async-done | bytes 2097168 | tf_op jit(solution)/shard_map/psum | solution.py:154
  440.5 2.4 broadcast_multiply_fusion.1
  443.0 1.1 broadcast_multiply_fusion
  (77 shorter events, 12.7 us)
Async XLA Ops:
  7.2 28.0 %copy-start = (bf16[256,1024]{1,0:T(8,128)(2,1)S(1)}, bf16[256,1024]{1,0:T(8,128)(2,1)}, u32[]{:S(2)}) copy-start(bf16[256,1024]{1,0:T(8,128)(2,1)} %param.19) | copy-start | bytes 1572868
  7.2 24.1 %copy-start.1 = (bf16[1,6,64,256]{3,2,1,0:T(8,128)(2,1)S(1)}, bf16[1,6,64,256]{3,2,1,0:T(8,128)(2,1)}, u32[]{:S(2)}) copy-start(bf16[1,6,64,256]{3,2,1,0:T(8,128)(2,1)} %param.12) | copy-start | bytes 589828
  7.2 24.1 %copy-start.8 = (f32[256]{0:T(256)S(1)}, f32[256]{0:T(256)}, u32[]{:S(2)}) copy-start(f32[256]{0:T(256)} %param.16) | copy-start | bytes 3076
  7.2 433.3 %all-reduce.4.cloned.1.call-start = ((), (), s32[]{:S(2)}) async-start(), calls=%async_computation | async-start | bytes 4194304 | tf_op jit(solution)/shard_map/psum | solution.py:154
  8.1 15.3 %collective-permute-start.1 = (bf16[1,6,3,256]{3,2,1,0:T(4,128)(2,1)S(1)}, bf16[1,6,3,256]{3,2,1,0:T(4,128)(2,1)S(1)}, u32[]{:S(2)}, u32[]{:S(2)}) collective-permute-start(bf16[1,6,3,256]{3,2,1,0:T(4,128)(2,1)S(1)} %get-tuple-element.102), channel_id=1, source_target_pairs={{64,0},{128,64},{192,128},{256,192},{320,256},{384,320},{448,384},... | collective-permute-start | bytes 27656 | tf_op jit(solution)/shard_map/ppermute | solution.py:15
  16.9 6.5 %collective-permute-start = (bf16[1,6,3,256]{3,2,1,0:T(4,128)(2,1)S(1)}, bf16[1,6,3,256]{3,2,1,0:T(4,128)(2,1)S(1)}, u32[]{:S(2)}, u32[]{:S(2)}) collective-permute-start(bf16[1,6,3,256]{3,2,1,0:T(4,128)(2,1)S(1)} %get-tuple-element.101), channel_id=1, source_target_pairs={{0,64},{64,128},{128,192},{192,256},{256,320},{320,384},{384,448},... | collective-permute-start | bytes 27656 | tf_op jit(solution)/shard_map/ppermute | solution.py:14
  24.5 3.0 collective-permute-start.2
  25.8 5.5 %collective-permute-start.3 = (bf16[1,3,70,256]{3,2,1,0:T(8,128)(2,1)S(1)}, bf16[1,3,70,256]{3,2,1,0:T(8,128)(2,1)S(1)}, u32[]{:S(2)}, u32[]{:S(2)}) collective-permute-start(bf16[1,3,70,256]{3,2,1,0:T(8,128)(2,1)S(1)} %get-tuple-element.96), channel_id=1, source_target_pairs={{1,0},{2,1},{3,2},{4,3},{5,4},{6,5},{7,6},{8,7},{9,8},{10,9},{11,1... | collective-permute-start | bytes 322568 | tf_op jit(solution)/shard_map/ppermute | solution.py:15
  31.4 3.6 copy-start.5
  31.4 3.6 copy-start.7
  31.4 3.8 copy-start.4
  34.6 1.0 copy-start.9
  34.6 1.0 copy-start.10
  35.7 0.9 copy-start.3
  35.7 0.9 copy-start.6
  44.4 122.7 %collective-permute-start.4 = (bf16[1,6,3,256]{3,2,1,0:T(4,128)(2,1)S(1)}, bf16[1,6,3,256]{3,2,1,0:T(4,128)(2,1)S(1)}, u32[]{:S(2)}, u32[]{:S(2)}) collective-permute-start(bf16[1,6,3,256]{3,2,1,0:T(4,128)(2,1)S(1)} %get-tuple-element.100), channel_id=1, source_target_pairs={{0,64},{64,128},{128,192},{192,256},{256,320},{320,384},{384,448},... | collective-permute-start | bytes 27656 | tf_op jit(solution)/shard_map/ppermute | solution.py:14
  48.0 119.0 %collective-permute-start.5 = (bf16[1,6,3,256]{3,2,1,0:T(4,128)(2,1)S(1)}, bf16[1,6,3,256]{3,2,1,0:T(4,128)(2,1)S(1)}, u32[]{:S(2)}, u32[]{:S(2)}) collective-permute-start(bf16[1,6,3,256]{3,2,1,0:T(4,128)(2,1)S(1)} %get-tuple-element.99), channel_id=1, source_target_pairs={{64,0},{128,64},{192,128},{256,192},{320,256},{384,320},{448,384},... | collective-permute-start | bytes 27656 | tf_op jit(solution)/shard_map/ppermute | solution.py:15
  167.1 5.9 %collective-permute-start.6 = (bf16[1,3,70,256]{3,2,1,0:T(8,128)(2,1)S(1)}, bf16[1,3,70,256]{3,2,1,0:T(8,128)(2,1)S(1)}, u32[]{:S(2)}, u32[]{:S(2)}) collective-permute-start(bf16[1,3,70,256]{3,2,1,0:T(8,128)(2,1)S(1)} %get-tuple-element.91), channel_id=1, source_target_pairs={{1,0},{2,1},{3,2},{4,3},{5,4},{6,5},{7,6},{8,7},{9,8},{10,9},{11,1... | collective-permute-start | bytes 322568 | tf_op jit(solution)/shard_map/ppermute | solution.py:15
  168.4 5.7 %collective-permute-start.7 = (bf16[1,3,70,256]{3,2,1,0:T(8,128)(2,1)S(1)}, bf16[1,3,70,256]{3,2,1,0:T(8,128)(2,1)S(1)}, u32[]{:S(2)}, u32[]{:S(2)}) collective-permute-start(bf16[1,3,70,256]{3,2,1,0:T(8,128)(2,1)S(1)} %get-tuple-element.92), channel_id=1, source_target_pairs={{0,1},{1,2},{2,3},{3,4},{4,5},{5,6},{6,7},{7,8},{8,9},{9,10},{10,1... | collective-permute-start | bytes 322568 | tf_op jit(solution)/shard_map/ppermute | solution.py:14
  440.5 2.4 copy-start.2
Sparse Core Ops, SparseCore 0:
  167.1 273.3 all-reduce.3
where the time goes:
time: 452 us; the launch traced here: 451 us
  waiting for transfers between devices  268 us (59%)
  blocking collectives  112 us (25%)
  starting transfers between devices  24.9 us (6%)
  other arithmetic  20.3 us (4%)
  between operations  14.4 us (3%)
  matrix products  5.94 us (1%)
  local copies, waits for them, and re-layouts  5.65 us (1%)
    psum x1, waiting for transfers between devices, local(): lax.psum((grad_w_in, grad_w_out, grad_b_in, grad_b_out, grad_scale, grad_...  262 us
    psum x1, blocking collectives, local(): lax.psum((grad_w_in, grad_w_out, grad_b_in, grad_b_out, grad_scale, grad_...  112 us
    ppermute x4, starting transfers between devices, extended(): after = lax.ppermute(leading, axis, down)  14 us
    ppermute x4, starting transfers between devices, extended(): before = lax.ppermute(last, axis, up)  10.9 us
  transfers between devices with their start and end apart: 9, of which 4 were waited for; matrix products, arithmetic and copies ran while one was open for 3% of the time, Pallas kernels for 0%

commit v1 on v0

--- a/solution.py
+++ b/solution.py
@@ -152,18 +152,21 @@
         grad_terms
     )
     reduced = lax.psum(
-        (
-            grad_w_in,
-            grad_w_out,
-            grad_b_in,
-            grad_b_out,
-            grad_scale,
-            grad_ln_gain,
-            grad_ln_bias,
-            kernel_part,
-            bias_part,
+        lax.psum(
+            (
+                grad_w_in,
+                grad_w_out,
+                grad_b_in,
+                grad_b_out,
+                grad_scale,
+                grad_ln_gain,
+                grad_ln_bias,
+                kernel_part,
+                bias_part,
+            ),
+            "lon",
         ),
-        ("lon", "lat"),
+        "lat",
     )
     (
         grad_w_in,

time: 452 us -> 1370 us (3.03)
  the two profiles are of different devices: /device:TPU:1 before, /device:TPU:8 now
where the time goes in v1:
time: 1370 us
  waiting for transfers between devices  836 us (61%)
  blocking collectives  467 us (34%)
  other arithmetic  20.3 us (1%)
  starting transfers between devices  19.2 us (1%)
  between operations  14.4 us (1%)
    psum x1, waiting for transfers between devices, local(): lax.psum(lax.psum((grad_w_in, grad_w_out, grad_b_in, grad_b_out, grad_sca...  825 us
    psum x1, blocking collectives, local(): lax.psum(lax.psum((grad_w_in, grad_w_out, grad_b_in, grad_b_out, grad_sca...  440 us
  transfers between devices with their start and end apart: 10, of which 6 were waited for; matrix products, arithmetic and copies ran while one was open for 1% of the time, Pallas kernels for 0%

profile of v1, /device:TPU:8, one launch (start us, length us, event | category | flops | bytes accessed | tf_op | source)
XLA Modules:
  0.0 1367.7 jit_solution(10605783906825718013)
XLA Ops:
  8.1 1.9 collective-permute-start.1
  10.0 2.4 collective-permute-start
  14.4 1.0 fusion.149
  17.0 2.2 collective-permute-done
  19.2 1.0 pad_maximum_fusion.2
  20.3 2.1 collective-permute-start.2
  22.4 1.3 collective-permute-start.3
  23.7 1.9 collective-permute-done.2
  25.6 4.8 collective-permute-done.3
  30.4 3.2 fusion.142
  36.6 1.3 convert_reduce_fusion
  40.3 1.4 fusion.151
  41.7 1.7 fusion.141
  43.4 2.0 collective-permute-start.4
  45.4 3.5 collective-permute-start.5
  50.1 26.7 %all-reduce.2 = (f32[7,7,256]{2,1,0:T(8,128)S(1)}, f32[256]{0:T(256)S(1)}, f32[256]{0:T(256)S(1)}, f32[256]{0:T(256)S(1)}, f32[1024]{0:T(1024)S(1)}, /*index=5*/f32[256]{0:T(256)S(1)}, f32[256]{0:T(256)S(1)}) all-reduce(f32[7,7,256]{2,1,0:T(8,128)S(1)} %constant_dynamic-update-slice_fusion.2, ...), channel_id=1, replica_groups=mesh['lon'=8,'lat'=64] {'lon'}, use_global_device_ids=true, to_apply=%region_53.0 | all-reduce | flops 14848 | bytes 118784 | tf_op jit(solution)/shard_map/psum | solution.py:155
  76.8 439.9 %all-reduce = (f32[7,7,256]{2,1,0:T(8,128)S(1)}, f32[256]{0:T(256)S(1)}, f32[256]{0:T(256)S(1)}, f32[256]{0:T(256)S(1)}, f32[1024]{0:T(1024)S(1)}, /*index=5*/f32[256]{0:T(256)S(1)}, f32[256]{0:T(256)S(1)}) all-reduce(f32[7,7,256]{2,1,0:T(8,128)S(1)} %get-tuple-element.83, ...), channel_id=1, replica_groups=mesh['lon'=8,'lat'=64] {'lat'}, use_global_device_ids=true, to_apply=%region_54.0 | all-reduce | flops 14848 | bytes 118784 | tf_op jit(solution)/shard_map/psum | solution.py:154
  520.3 1.3 collective-permute-start.6
  521.6 4.6 collective-permute-start.7
  527.3 1.1 collective-permute-done.7
  528.5 3.8 fusion.55
  532.3 825.1 %all-reduce.7.cloned.1.call-done = (f32[256,1024]{1,0:T(8,128)}, f32[1024,256]{1,0:T(8,128)}) async-done(((f32[256,1024]{1,0:T(8,128)}, f32[1024,256]{1,0:T(8,128)}), (f32[256,1024]{1,0:T(8,128)}, f32[1024,256]{1,0:T(8,128)})) %all-reduce.7.cloned.1.call-update) | async-done | bytes 2097168 | tf_op jit(solution)/shard_map/psum | solution.py:154
  1357.4 2.4 broadcast_multiply_fusion.1
  1359.8 1.1 broadcast_multiply_fusion
  (81 shorter events, 15.7 us)
Async XLA Ops:
  7.2 27.0 %copy-start = (bf16[256,1024]{1,0:T(8,128)(2,1)S(1)}, bf16[256,1024]{1,0:T(8,128)(2,1)}, u32[]{:S(2)}) copy-start(bf16[256,1024]{1,0:T(8,128)(2,1)} %param.19) | copy-start | bytes 1572868
  7.2 23.1 %copy-start.1 = (bf16[1,6,64,256]{3,2,1,0:T(8,128)(2,1)S(1)}, bf16[1,6,64,256]{3,2,1,0:T(8,128)(2,1)}, u32[]{:S(2)}) copy-start(bf16[1,6,64,256]{3,2,1,0:T(8,128)(2,1)} %param.12) | copy-start | bytes 589828
  7.2 23.2 %copy-start.8 = (f32[256]{0:T(256)S(1)}, f32[256]{0:T(256)}, u32[]{:S(2)}) copy-start(f32[256]{0:T(256)} %param.16) | copy-start | bytes 3076
  7.2 511.2 %all-reduce.9.cloned.1.call-start = ((), (), s32[]{:S(2)}) async-start(), calls=%async_computation.1 | async-start | bytes 4194304 | tf_op jit(solution)/shard_map/psum | solution.py:155
  8.1 8.9 collective-permute-start.1
  10.0 9.2 collective-permute-start
  20.3 5.3 collective-permute-start.2
  22.4 8.0 collective-permute-start.3
  30.4 3.6 copy-start.5
  30.4 3.6 copy-start.7
  30.4 3.8 copy-start.4
  33.7 1.0 copy-start.9
  33.7 1.0 copy-start.10
  34.7 0.9 copy-start.3
  34.7 0.9 copy-start.6
  43.4 476.8 %collective-permute-start.4 = (bf16[1,6,3,256]{3,2,1,0:T(4,128)(2,1)S(1)}, bf16[1,6,3,256]{3,2,1,0:T(4,128)(2,1)S(1)}, u32[]{:S(2)}, u32[]{:S(2)}) collective-permute-start(bf16[1,6,3,256]{3,2,1,0:T(4,128)(2,1)S(1)} %get-tuple-element.109), channel_id=1, source_target_pairs={{0,64},{64,128},{128,192},{192,256},{256,320},{320,384},{384,448},... | collective-permute-start | bytes 27656 | tf_op jit(solution)/shard_map/ppermute | solution.py:14
  45.4 474.7 %collective-permute-start.5 = (bf16[1,6,3,256]{3,2,1,0:T(4,128)(2,1)S(1)}, bf16[1,6,3,256]{3,2,1,0:T(4,128)(2,1)S(1)}, u32[]{:S(2)}, u32[]{:S(2)}) collective-permute-start(bf16[1,6,3,256]{3,2,1,0:T(4,128)(2,1)S(1)} %get-tuple-element.108), channel_id=1, source_target_pairs={{64,0},{128,64},{192,128},{256,192},{320,256},{384,320},{448,384},... | collective-permute-start | bytes 27656 | tf_op jit(solution)/shard_map/ppermute | solution.py:15
  49.8 1307.6 %all-reduce.7.cloned.1.call-start = ((), (), s32[]{:S(2)}) async-start(), calls=%async_computation | async-start | bytes 4194304 | tf_op jit(solution)/shard_map/psum | solution.py:154
  520.3 7.0 collective-permute-start.6
  521.6 6.9 collective-permute-start.7
  1357.4 2.4 copy-start.2
Sparse Core Ops, SparseCore 0:
  49.9 96.1 all-reduce.8
  518.5 838.8 all-reduce.6
